TPU v7x, 32 devices: a whole 2x2x4 slice. The times are simulated.
32 devices in a mesh: beam: 2 (over x), band: 2 (over core), tm: 8 (over z, y).
Axes of the slice: x: 2, y: 2, z: 4, core: 2. Of those that a mesh axis runs over, the one named last changes fastest.
Arguments:
- samples: bfloat16 [2048, 32768], P(('beam', 'band'), 'tm'), parts along dimension 0, may hold values from -3 to 3
- clip_mask: int32 [2048, 256], P(('beam', 'band'), 'tm'), parts along dimension 0, may hold values 0 or 1
- delays: int32 [8, 1024], P(None, 'band'), may hold values from 0 to 4095
- templates: bfloat16 [2, 64, 1024], replicated, may hold values from -0.125 to 0.125
Outputs:
- powers: float32 [16, 64, 16384], P(('beam', 'tm'), None, 'band'), parts along dimension 0
There are 2 independent parts, one for each index of `beam`. A program takes and returns all parts, laid end to end along the dimension named above; an argument that names none is the same for every part. Nothing has to cross between parts.
All inputs are finite; a program needn't handle non-finite values. No bound on the sum of `clip_mask` on one device may be relied on, other than what follows from the above.
Results may differ from a plain program's by a relative error of at most 0.0095.
Values may be sent and summed in bfloat16 or wider, within the bound.
A program may use at most 192 MiB of HBM per device.

v0:
```python
import math

import jax
import jax.numpy as jnp
from jax import lax
from jax.experimental import pallas as pl
from jax.experimental.pallas import tpu as pltpu
from jax.sharding import PartitionSpec as P

CHANNELS = 1024
SEARCH = 16384
LANES = 128

clip_level = 2.5
fine = lax.Precision.HIGH


def counting(length):
    return jnp.arange(length, dtype=jnp.int32)


def phase_table(first_index, second_index, period):
    turn_count = first_index[:, None] * second_index[None, :] % period
    angles = turn_count.astype(jnp.float32) * (2.0 * math.pi / period)
    return (jnp.cos(angles), jnp.sin(angles))


def dedisperse(samples, clip_mask, delays):
    chan_count, slab_len = samples.shape
    rows = slab_len // LANES
    dm_count = delays.shape[0]
    block = 128
    steps = chan_count // block
    padded_len = 2 * slab_len
    scale = 1.0 / math.sqrt(CHANNELS)
    assert clip_mask.shape[1] == rows
    lane_bits = LANES.bit_length() - 1

    def kernel(delay_ref, sample_ref, mask_ref, out_ref, wrapped_ref, total_ref):
        step = pl.program_id(0)

        @pl.when(step == 0)
        def _():
            total_ref[...] = jnp.zeros_like(total_ref)

        flags = mask_ref[...]
        for chan in range(block):
            values = jnp.clip(sample_ref[chan].astype(jnp.float32), -clip_level, clip_level)
            values = values * flags[:, chan : chan + 1]
            wrapped_ref[chan * 2 * rows : chan * 2 * rows + rows, :] = values
            wrapped_ref[chan * 2 * rows + rows : (chan + 1) * 2 * rows, :] = values

        lane = lax.broadcasted_iota(jnp.int32, (rows, LANES), 1)
        index = lax.broadcasted_iota(jnp.int32, (rows, LANES), 0) * LANES + lane
        from_end = LANES - 1 - lane[:16]

        def one_dm(dm, _):
            chan_base = dm * chan_count + step * block

            def one_channel(chan, sums):
                both, own = sums
                delay = delay_ref[chan_base + chan]
                low = delay & (LANES - 1)
                start = chan * (2 * rows) + (rows - 1) - (delay >> lane_bits)
                keep = from_end >= low
                new_both, new_own = [], []
                before = wrapped_ref[pl.ds(start, rows), :]
                same = wrapped_ref[pl.ds(start + 1, rows), :]
                for r in range(rows // 16):
                    pair = slice(16 * r, 16 * r + 16)
                    merged = jnp.where(keep, same[pair], before[pair]).astype(jnp.bfloat16)
                    rolled = pltpu.roll(merged, low, 1).astype(jnp.float32)
                    for h in range(2):
                        moved = rolled[8 * h : 8 * h + 8]
                        t = 2 * r + h
                        new_both.append(both[t] + moved)
                        new_own.append(
                            own[t] + jnp.where(index[8 * t : 8 * t + 8] >= delay, moved, 0.0)
                        )
                return (tuple(new_both), tuple(new_own))

            tiles = [slice(8 * r, 8 * r + 8) for r in range(rows // 8)]
            both, own = lax.fori_loop(
                0,
                block,
                one_channel,
                (
                    tuple(total_ref[dm, 0, t, :] for t in tiles),
                    tuple(total_ref[dm, 1, t, :] for t in tiles),
                ),
                unroll=block,
            )
            for t, x, y in zip(tiles, both, own):
                total_ref[dm, 0, t, :] = x
                total_ref[dm, 1, t, :] = y
            return 0

        lax.fori_loop(0, dm_count, one_dm, 0)

        @pl.when(step == steps - 1)
        def _():
            sign = (1 - 2 * (lane % 2)).astype(jnp.float32)

            def finish(dm, _):
                both = total_ref[dm, 0]
                own = total_ref[dm, 1]
                half_rate = jnp.sum(both * sign) * sign * (1.0 / padded_len)
                out_ref[dm, :rows, :] = ((own - half_rate) * scale).astype(out_ref.dtype)
                out_ref[dm, rows:, :] = ((both - own - half_rate) * scale).astype(out_ref.dtype)
                return 0

            lax.fori_loop(0, dm_count, finish, 0)

    return pl.pallas_call(
        kernel,
        out_shape=jax.ShapeDtypeStruct((dm_count, 2 * rows, LANES), jnp.bfloat16),
        grid_spec=pltpu.PrefetchScalarGridSpec(
            num_scalar_prefetch=1,
            grid=(steps,),
            in_specs=[
                pl.BlockSpec((block, rows, LANES), lambda i, *_: (i, 0, 0)),
                pl.BlockSpec((rows, block), lambda i, *_: (0, i)),
            ],
            out_specs=pl.BlockSpec((dm_count, 2 * rows, LANES), lambda i, *_: (0, 0, 0)),
            scratch_shapes=[
                pltpu.VMEM((block * 2 * rows, LANES), jnp.float32),
                pltpu.VMEM((dm_count, 2, rows, LANES), jnp.float32),
            ],
        ),
        compiler_params=pltpu.CompilerParams(vmem_limit_bytes=48 << 20),
    )(
        delays.reshape(-1),
        samples.reshape(chan_count, rows, LANES),
        clip_mask.T.astype(jnp.float32),
    )


def gather_series(partial_value):
    tm_count = lax.axis_size("tm")
    band_count = lax.axis_size("band")
    _, padded_rows, _ = partial_value.shape
    rows = padded_rows // 2
    mesh_ids = pl.DeviceIdType.MESH

    def kernel(part_ref, out_ref, held_ref, sent, arrived, passed, received, local_sem):
        me = lax.axis_index("tm")
        band = lax.axis_index("band")

        def device(tm, core):
            return {"tm": tm, "band": core}

        barrier = pltpu.get_barrier_semaphore()
        for k in range(1, tm_count):
            pl.semaphore_signal(
                barrier, 1, device_id=device(lax.rem(me + k, tm_count), band), device_id_type=mesh_ids
            )
        for j in range(1, band_count):
            pl.semaphore_signal(
                barrier, 1, device_id=device(me, lax.rem(band + j, band_count)), device_id_type=mesh_ids
            )
        pl.semaphore_wait(barrier, tm_count + band_count - 2)

        outgoing = []
        for k in range(1, tm_count):
            target = lax.rem(me + k, tm_count)
            copy = pltpu.make_async_remote_copy(
                src_ref=part_ref.at[target],
                dst_ref=held_ref.at[band, me],
                send_sem=sent.at[k],
                recv_sem=arrived.at[k],
                device_id=device(target, band),
                device_id_type=mesh_ids,
            )
            copy.start()
            outgoing.append(copy)
        kept = pltpu.make_async_copy(part_ref.at[me], held_ref.at[band, me], local_sem)
        kept.start()
        handed = []

        def hand_on(source, piece, slot):
            for j in range(1, band_count):
                copy = pltpu.make_async_remote_copy(
                    src_ref=piece,
                    dst_ref=held_ref.at[band, source],
                    send_sem=passed.at[slot, j],
                    recv_sem=received.at[slot, j],
                    device_id=device(me, lax.rem(band + j, band_count)),
                    device_id_type=mesh_ids,
                )
                copy.start()
                handed.append(copy)

        hand_on(me, part_ref.at[me], 0)
        for k in range(1, tm_count):
            outgoing[k - 1].wait_recv()
            source = lax.rem(me + tm_count - k, tm_count)
            hand_on(source, held_ref.at[band, source], k)
        for copy in outgoing:
            copy.wait_send()
        kept.wait()
        for copy in handed:
            copy.wait()

        tail = jnp.zeros((rows, LANES), jnp.float32)
        for s in range(tm_count):
            piece = held_ref[0, s].astype(jnp.float32)
            for b in range(1, band_count):
                piece = piece + held_ref[b, s].astype(jnp.float32)
            out_ref[s * rows : (s + 1) * rows, :] = piece[:rows] + tail
            tail = piece[rows:]

    return pl.pallas_call(
        kernel,
        out_shape=jax.ShapeDtypeStruct((tm_count * rows, LANES), jnp.float32),
        in_specs=[pl.BlockSpec(memory_space=pltpu.VMEM)],
        out_specs=pl.BlockSpec(memory_space=pltpu.VMEM),
        scratch_shapes=[
            pltpu.VMEM((band_count, tm_count, padded_rows, LANES), jnp.bfloat16),
            pltpu.SemaphoreType.DMA((tm_count,)),
            pltpu.SemaphoreType.DMA((tm_count,)),
            pltpu.SemaphoreType.DMA((tm_count, band_count)),
            pltpu.SemaphoreType.DMA((tm_count, band_count)),
            pltpu.SemaphoreType.DMA,
        ],
        compiler_params=pltpu.CompilerParams(collective_id=0, has_side_effects=True),
    )(partial_value)


def correlate(framed, templates, bin_count):
    tmpl_count, tap_len = templates.shape[1:]
    blocks = tap_len // LANES
    frame_len = framed.shape[1]
    width = 1024
    steps = bin_count // width

    def kernel(framed_ref, tmpl_ref, out_ref, taps_ref, shifted_ref):
        step = pl.program_id(0)

        @pl.when(step == 0)
        def _():
            row = lax.broadcasted_iota(jnp.int32, (LANES, LANES), 0)
            col = lax.broadcasted_iota(jnp.int32, (LANES, LANES), 1)
            flip = (row + col == LANES - 1).astype(jnp.bfloat16)
            for b in range(blocks):
                cut = slice(b * LANES, (b + 1) * LANES)
                real = jnp.dot(tmpl_ref[0, :, cut], flip, preferred_element_type=jnp.float32)
                imag = jnp.dot(tmpl_ref[1, :, cut], flip, preferred_element_type=jnp.float32)
                taps_ref[b, :tmpl_count, :LANES] = real.astype(jnp.bfloat16)
                taps_ref[b, :tmpl_count, LANES:] = (-imag).astype(jnp.bfloat16)
                taps_ref[b, tmpl_count:, :LANES] = imag.astype(jnp.bfloat16)
                taps_ref[b, tmpl_count:, LANES:] = real.astype(jnp.bfloat16)
            for part in range(2):
                spread = jnp.broadcast_to(framed_ref[part : part + 1, :], (8, frame_len))
                base = pltpu.roll(spread, 0, 1, stride=1, stride_axis=0)
                for g in range(LANES // 16):
                    lower = base if g == 0 else pltpu.roll(base, 16 * g, 1)
                    upper = pltpu.roll(base, 16 * g + 8, 1)
                    start = part * LANES + 16 * g
                    shifted_ref[start : start + 16, :] = jnp.concatenate(
                        [lower, upper], axis=0
                    ).astype(jnp.bfloat16)

        total = jnp.zeros((2 * tmpl_count, width), jnp.float32)
        for b in range(blocks):
            first = pl.multiple_of(step * width + (b + 1) * LANES, LANES)
            total = total + jnp.dot(
                taps_ref[b], shifted_ref[:, pl.ds(first, width)], preferred_element_type=jnp.float32
            )
        out_ref[0] = jnp.square(total[:tmpl_count]) + jnp.square(total[tmpl_count:])

    return pl.pallas_call(
        kernel,
        out_shape=jax.ShapeDtypeStruct((1, tmpl_count, bin_count), jnp.float32),
        grid=(steps,),
        in_specs=[
            pl.BlockSpec((2, frame_len), lambda i: (0, 0)),
            pl.BlockSpec(templates.shape, lambda i: (0, 0, 0)),
        ],
        out_specs=pl.BlockSpec((1, tmpl_count, width), lambda i: (0, 0, i)),
        scratch_shapes=[
            pltpu.VMEM((blocks, 2 * tmpl_count, 2 * LANES), jnp.bfloat16),
            pltpu.VMEM((2 * LANES, frame_len), jnp.bfloat16),
        ],
        compiler_params=pltpu.CompilerParams(vmem_limit_bytes=48 << 20),
    )(framed, templates)


def local(samples, clip_mask, delays, templates):
    partial_value = dedisperse(samples, clip_mask, delays)
    whole = gather_series(partial_value)
    return search(whole, templates)


def search(whole, templates):
    row_count, inner_len = whole.shape
    total_len = row_count * inner_len
    bin_cols = SEARCH // row_count
    scale_bins = 1.0 / math.sqrt(total_len)
    outer_cos, outer_sin = phase_table(counting(row_count), counting(row_count), row_count)
    table_outer = jnp.concatenate([outer_cos, -outer_sin], axis=0)
    hold_cos, hold_sin = phase_table(counting(row_count), counting(inner_len), total_len)
    own_cols = bin_cols // lax.axis_size("band")
    folded = jnp.dot(table_outer, whole, precision=fine)
    fold_real = folded[:row_count]
    fold_imag = folded[row_count:]
    hold_real = fold_real * hold_cos + fold_imag * hold_sin
    hold_imag = fold_imag * hold_cos - fold_real * hold_sin
    half_taps = templates.shape[2] // 2
    side_cols = -(-half_taps // row_count)
    cols = lax.axis_index("band") * own_cols - side_cols + counting(own_cols + 2 * side_cols)
    last_cos, last_sin = phase_table(counting(inner_len), cols % inner_len, inner_len)
    inside = ((cols >= 0) & (cols < bin_cols)).astype(jnp.float32) * scale_bins
    last_cos = last_cos * inside
    last_sin = last_sin * inside
    table_last = jnp.concatenate(
        [
            jnp.concatenate([last_cos, -last_sin], axis=1),
            jnp.concatenate([last_sin, last_cos], axis=1),
        ],
        axis=0,
    )
    out = jnp.dot(jnp.concatenate([hold_real, hold_imag], axis=1), table_last, precision=fine)
    ordered = out.T.reshape(2, -1)
    local_bins = own_cols * row_count
    skip = side_cols * row_count - half_taps
    if skip:
        framed = ordered[:, skip - 1 : skip - 1 + local_bins + 2 * half_taps]
    else:
        framed = jnp.pad(ordered[:, :-1], ((0, 0), (1, 0)))
    return correlate(framed, templates, local_bins)


def solution(mesh):
    in_specs = (P(("beam", "band"), "tm"), P(("beam", "band"), "tm"), P(None, "band"), P())
    out_specs = P(("beam", "tm"), None, "band")
    return jax.shard_map(local, mesh=mesh, in_specs=in_specs, out_specs=out_specs, check_vma=False)
```

profile of v0, /device:TPU:0, one launch (start us, length us, event | category | flops | bytes accessed | tf_op | source)
XLA Modules:
  0.0 52.3 jit_solution(13826376718982631405)
XLA Ops:
  0.0 0.7 %copy.5 = s32[1,4,8,128]{3,1,2,0:T(4,128)S(1)} copy(s32[1,4,8,128]{3,2,1,0:T(8,128)} %bitcast.12) | data formatting | bytes 32768
  0.7 0.0 copy-start.2
  0.7 3.5 %copy.6 = bf16[64,8,32,128]{3,2,1,0:T(8,128)(2,1)S(1)} copy(bf16[64,8,32,128]{3,1,2,0:T(8,128)(2,1)} %bitcast.10) | data formatting | bytes 8388608
  4.2 0.0 copy-start.1
  4.2 0.0 copy-done.2
  4.2 23.3 %shard_map.46.part_ref = bf16[8,64,128]{2,1,0:T(8,128)(2,1)S(1)} custom-call(s32[4096]{0:T(1024)S(1)} %bitcast.9, bf16[512,32,128]{2,1,0:T(8,128)(2,1)S(1)} %bitcast.8, f32[32,512]{1,0:T(8,128)S(1)} %convert_bitcast_fusion.mask_ref), custom_call_target="tpu_custom_call" | custom-call | tf_op jit(solution)/shard_map/pallas_call | solution.py:114
  27.5 0.0 copy-start
  27.5 0.6 %copy-done = bf16[8,64,128]{2,1,0:T(8,128)(2,1)} copy-done((bf16[8,64,128]{2,1,0:T(8,128)(2,1)}, bf16[8,64,128]{2,1,0:T(8,128)(2,1)S(1)}, u32[]{:S(2)}) %copy-start) | copy-done | bytes 131096
  28.2 12.2 %shard_map.47 = f32[256,128]{1,0:T(8,128)} custom-call(bf16[8,64,128]{2,1,0:T(8,128)(2,1)} %copy-done), custom_call_target="tpu_custom_call" | custom-call | tf_op jit(solution)/shard_map/pallas_call | solution.py:212
  40.4 1.0 %sine_negate_fusion = (f32[256,256]{1,0:T(8,128)S(1)}, f32[256,256]{1,0:T(8,128)S(1)}) fusion(), kind=kLoop, calls=%fused_computation.14 | loop fusion | flops 983040 | bytes 524288 | tf_op jit(solution)/shard_map/neg | solution.py:300
  41.4 1.3 %fusion = f32[512,128]{0,1:T(8,128)S(1)} fusion(f32[256,128]{1,0:T(8,128)} %shard_map.47, f32[256,256]{1,0:T(8,128)S(1)} %get-tuple-element.10, f32[256,256]{1,0:T(8,128)S(1)} %get-tuple-element.11), kind=kOutput, calls=%fused_computation | convolution fusion | flops 100794368 | bytes 917504 | tf_op jit(solution)/shard_map/dot_general | solution.py:303
  42.7 0.6 %multiply_add_fusion = (f32[256,128]{0,1:T(8,128)S(1)}, f32[256,128]{0,1:T(8,128)S(1)}) fusion(f32[512,128]{0,1:T(8,128)S(1)} %fusion), kind=kLoop, calls=%fused_computation.25 | loop fusion | flops 655360 | bytes 524288 | tf_op jit(solution)/shard_map/add | solution.py:306
  43.3 0.2 fusion.36
  43.5 0.2 fusion.7
  43.8 0.1 pad.4.framed_ref
  43.9 0.0 copy-done.1
  43.9 8.4 %shard_map.48 = f32[1,64,8192]{2,1,0:T(8,128)} custom-call(f32[2,9216]{1,0:T(2,128)S(1)} %pad.4.framed_ref, bf16[2,64,1024]{2,1,0:T(8,128)(2,1)S(1)} %copy-done.1), custom_call_target="tpu_custom_call" | custom-call | tf_op jit(solution)/shard_map/pallas_call | solution.py:271
  (4 shorter events, 0.1 us)
Async XLA Ops:
  0.7 3.5 %copy-start.2 = (s32[512,32]{0,1:T(8,128)S(1)}, s32[512,32]{0,1:T(8,128)}, u32[]{:S(2)}) copy-start(s32[512,32]{0,1:T(8,128)} %param.5) | copy-start | bytes 196612
  4.2 39.7 %copy-start.1 = (bf16[2,64,1024]{2,1,0:T(8,128)(2,1)S(1)}, bf16[2,64,1024]{2,1,0:T(8,128)(2,1)}, u32[]{:S(2)}) copy-start(bf16[2,64,1024]{2,1,0:T(8,128)(2,1)} %tmpl_ref.1) | copy-start | bytes 786436
  27.5 0.7 %copy-start = (bf16[8,64,128]{2,1,0:T(8,128)(2,1)}, bf16[8,64,128]{2,1,0:T(8,128)(2,1)S(1)}, u32[]{:S(2)}) copy-start(bf16[8,64,128]{2,1,0:T(8,128)(2,1)S(1)} %shard_map.46.part_ref) | copy-start | bytes 393220
where the time goes:
time: 52.6 us; the launch traced here: 52.3 us
  Pallas kernels  43.9 us (83%)
  local copies, waits for them, and re-layouts  5.02 us (10%)
  other arithmetic  1.79 us (3%)
  matrix products  1.53 us (3%)
    pallas_call x1, Pallas kernels, dedisperse(): pl.pallas_call(kernel, out_shape=jax.ShapeDtypeStruct((dm_count, 2 * rows...  23.3 us
    pallas_call x1, Pallas kernels, gather_series(): pl.pallas_call(kernel, out_shape=jax.ShapeDtypeStruct((tm_count * rows, L...  12.2 us
    pallas_call x1, Pallas kernels, correlate(): pl.pallas_call(kernel, out_shape=jax.ShapeDtypeStruct((1, tmpl_count, bin...  8.41 us
    unnamed x8, local copies, waits for them, and re-layouts  4.84 us
    dot_general x1, matrix products, search(): folded = jnp.dot(table_outer, whole, precision=fine)  1.32 us

commit v1 on v0

v1 whole, which is shorter than its diff:
```python
import math

import jax
import jax.numpy as jnp
from jax import lax
from jax.experimental import pallas as pl
from jax.experimental.pallas import tpu as pltpu
from jax.sharding import PartitionSpec as P

CHANNELS = 1024
SEARCH = 16384
LANES = 128

clip_level = 2.5
fine = lax.Precision.HIGH


def counting(length):
    return jnp.arange(length, dtype=jnp.int32)


def phase_table(first_index, second_index, period):
    turn_count = first_index[:, None] * second_index[None, :] % period
    angles = turn_count.astype(jnp.float32) * (2.0 * math.pi / period)
    return (jnp.cos(angles), jnp.sin(angles))


def dedisperse(samples, clip_mask, delays):
    chan_count, slab_len = samples.shape
    rows = slab_len // LANES
    dm_count = delays.shape[0]
    tm_count = lax.axis_size("tm")
    band_count = lax.axis_size("band")
    padded_len = 2 * slab_len
    scale = 1.0 / math.sqrt(CHANNELS)
    assert clip_mask.shape[1] == rows and dm_count == tm_count
    mesh_ids = pl.DeviceIdType.MESH
    lane_bits = LANES.bit_length() - 1
    pitch = rows + 8
    width = 2 * LANES
    chunks = slab_len // width
    group = width // rows
    block = 64
    spans = chan_count // LANES
    padded_rows = 2 * rows

    def kernel(
        delay_ref, lag_ref, sample_ref, mask_ref, out_ref,
        held_in, natural, same_ref, before_ref, flag_ref, lag_rows, carry_ref, part_ref, held_ref,
        load_sem, sent, arrived,
    ):
        me = lax.axis_index("tm")
        band = lax.axis_index("band")

        def load(j):
            start = pl.multiple_of(j * width, width)
            cut = pl.ds(start, width)
            return pltpu.make_async_copy(sample_ref.at[:, cut], held_in.at[:, cut], load_sem.at[j])

        for j in range(chunks):
            load(j).start()

        barrier = pltpu.get_barrier_semaphore()
        peers = tm_count * band_count - 1
        place = me * band_count + band

        def greet(k, _):
            other = lax.rem(place + k, peers + 1)
            pl.semaphore_signal(
                barrier, 1,
                device_id={"tm": other // band_count, "band": lax.rem(other, band_count)},
                device_id_type=mesh_ids,
            )
            return 0

        lax.fori_loop(1, peers + 1, greet, 0)

        flag_ref[...] = mask_ref[...].astype(jnp.float32).T.astype(jnp.bfloat16)
        spread_lane = lax.broadcasted_iota(jnp.int32, (LANES, rows * LANES), 1)
        spread_row = lax.broadcasted_iota(jnp.int32, (LANES, rows * LANES), 0)
        spread = (spread_lane // rows == spread_row).astype(jnp.float32).astype(jnp.bfloat16)
        row_lags = (lag_ref[...] >> lane_bits).astype(jnp.float32).astype(jnp.bfloat16)
        for i in range(spans):
            lag_rows[i] = jnp.dot(
                row_lags[:, i * LANES : (i + 1) * LANES], spread, preferred_element_type=jnp.float32
            )

        def take(j, _):
            load(j).wait()
            start = pl.multiple_of(j * width, width)
            first = lax.broadcasted_iota(jnp.int32, (rows, width), 0) - 2 * j
            which = lax.broadcasted_iota(jnp.int32, (rows, width), 1) // LANES
            pick = (first == which).astype(jnp.float32).astype(jnp.bfloat16)
            flags = jnp.dot(flag_ref[...], pick, preferred_element_type=jnp.float32)
            for g in range(chan_count // 16):
                values = held_in[16 * g : 16 * g + 16, pl.ds(start, width)]
                values = jnp.clip(values, -clip_level, clip_level).astype(jnp.float32)
                values = values * flags[16 * g : 16 * g + 16]
                for h in range(2):
                    for t in range(2):
                        natural[pl.ds((16 * g + 8 * t) * pitch + 8 + 2 * j + h, 8, stride=pitch), :] = (
                            values[8 * t : 8 * t + 8, h * LANES : (h + 1) * LANES]
                        )
            return 0

        lax.fori_loop(0, chunks, take, 0)

        def pack(i, _):
            base = pl.multiple_of(i * (8 * pitch), 8)
            last = natural[pl.ds(base + pitch - 1, 8, stride=pitch), :]
            natural[pl.ds(base + 7, 8, stride=pitch), :] = last
            for c in range(8):
                target = pl.multiple_of(i * (8 * rows) + c * rows, rows)
                same_ref[pl.ds(target, rows), :] = natural[
                    pl.ds(base + c * pitch + 8, rows), :
                ].astype(jnp.bfloat16)
                before_ref[pl.ds(target, rows), :] = natural[
                    pl.ds(base + c * pitch + 7, rows), :
                ].astype(jnp.bfloat16)
            return 0

        lax.fori_loop(0, chan_count // 8, pack, 0)

        lane = lax.broadcasted_iota(jnp.int32, (rows, LANES), 1)
        lane_half = lane.astype(jnp.float32).astype(jnp.bfloat16)
        row_lane = lax.broadcasted_iota(jnp.int32, (1, LANES), 1)
        sign = (1 - 2 * (lax.broadcasted_iota(jnp.int32, (padded_rows, LANES), 1) % 2)).astype(jnp.float32)
        apart = (
            lax.broadcasted_iota(jnp.int32, (padded_rows, width), 0)
            - lax.broadcasted_iota(jnp.int32, (padded_rows, width), 1) % rows
        ).astype(jnp.float32)

        def piece(k, j):
            target = lax.rem(me + 1 + k, tm_count)
            return pltpu.make_async_remote_copy(
                src_ref=part_ref.at[target],
                dst_ref=held_ref.at[band, me],
                send_sem=sent.at[k, j],
                recv_sem=arrived.at[k, j],
                device_id={"tm": target, "band": lax.rem(band + j, band_count)},
                device_id_type=mesh_ids,
            )

        def one_dm(k, _):
            dm = lax.rem(me + 1 + k, tm_count)

            def one_block(n, total):
                @pl.when((n == 1) & (k == 1))
                def _():
                    pl.semaphore_wait(barrier, peers)

                @pl.when((n == 1) & (k > 0))
                def _():
                    for j in range(band_count):
                        piece(k - 1, j).start()

                for b in range(block // group):
                    turned = []
                    for i in range(group):
                        chan = n * block + b * group + i
                        low = delay_ref[dm, chan] & (LANES - 1)
                        start = pl.multiple_of(chan * rows, rows)
                        edge = jnp.full((rows, LANES), (LANES - low).astype(jnp.float32)).astype(jnp.bfloat16)
                        merged = jnp.where(
                            lane_half < edge,
                            same_ref[pl.ds(start, rows), :],
                            before_ref[pl.ds(start, rows), :],
                        )
                        rolled = pltpu.roll(merged, low, 1)
                        top = rolled[:16].astype(jnp.float32)[:1]
                        carry_ref[pl.ds(chan, 1), :] = jnp.where(row_lane < low, top, 0.0)
                        turned.append(rolled)
                    place_in = pl.multiple_of(
                        lax.rem(n * block + b * group, LANES) * rows, width
                    )
                    lags = lag_rows[(n * block) // LANES, pl.ds(dm, 1), pl.ds(place_in, width)]
                    chosen = (apart == lags).astype(jnp.float32).astype(jnp.bfloat16)
                    total = total + jnp.dot(
                        chosen, jnp.concatenate(turned, axis=0), preferred_element_type=jnp.float32
                    )
                return total

            total = lax.fori_loop(
                0, chan_count // block, one_block, jnp.zeros((padded_rows, LANES), jnp.float32)
            )
            row = lax.broadcasted_iota(jnp.int32, (padded_rows, chan_count), 0)
            lags = lag_ref[pl.ds(dm, 1), :] >> lane_bits
            fix = (row == lags + rows).astype(jnp.float32) - (row == lags).astype(jnp.float32)
            total = total + jnp.dot(
                fix.astype(jnp.bfloat16),
                carry_ref[...].astype(jnp.bfloat16),
                preferred_element_type=jnp.float32,
            )
            half_rate = jnp.sum(total * sign) * sign * (1.0 / padded_len)
            result = ((total - half_rate) * scale).astype(jnp.bfloat16)
            part_ref[dm] = result

            @pl.when(k == dm_count - 1)
            def _():
                held_ref[band, me] = result

            return 0

        lax.fori_loop(0, dm_count, one_dm, 0)

        own = dm_count - 1
        for j in range(1, band_count):
            piece(own, j).start()
        for k in range(own):
            for j in range(band_count):
                piece(k, j).wait()
        for j in range(1, band_count):
            piece(own, j).wait()

        tail = jnp.zeros((rows, LANES), jnp.float32)
        for s in range(tm_count):
            piece_sum = held_ref[0, s].astype(jnp.float32)
            for b in range(1, band_count):
                piece_sum = piece_sum + held_ref[b, s].astype(jnp.float32)
            out_ref[s * rows : (s + 1) * rows, :] = piece_sum[:rows] + tail
            tail = piece_sum[rows:]

    vmem = pl.BlockSpec(memory_space=pltpu.VMEM)
    return pl.pallas_call(
        kernel,
        out_shape=jax.ShapeDtypeStruct((tm_count * rows, LANES), jnp.float32),
        in_specs=[
            pl.BlockSpec(memory_space=pltpu.SMEM),
            vmem,
            pl.BlockSpec(memory_space=pl.ANY),
            vmem,
        ],
        out_specs=vmem,
        scratch_shapes=[
            pltpu.VMEM((chan_count, slab_len), jnp.bfloat16),
            pltpu.VMEM((chan_count * pitch, LANES), jnp.float32),
            pltpu.VMEM((chan_count * rows, LANES), jnp.bfloat16),
            pltpu.VMEM((chan_count * rows, LANES), jnp.bfloat16),
            pltpu.VMEM((chan_count, rows), jnp.bfloat16),
            pltpu.VMEM((spans, dm_count, rows * LANES), jnp.float32),
            pltpu.VMEM((chan_count, LANES), jnp.float32),
            pltpu.VMEM((dm_count, padded_rows, LANES), jnp.bfloat16),
            pltpu.VMEM((band_count, tm_count, padded_rows, LANES), jnp.bfloat16),
            pltpu.SemaphoreType.DMA((chunks,)),
            pltpu.SemaphoreType.DMA((dm_count, band_count)),
            pltpu.SemaphoreType.DMA((dm_count, band_count)),
        ],
        compiler_params=pltpu.CompilerParams(
            collective_id=0, has_side_effects=True, vmem_limit_bytes=56 << 20
        ),
    )(delays, delays, samples, clip_mask.T)


def correlate(framed, templates, bin_count):
    tmpl_count, tap_len = templates.shape[1:]
    blocks = tap_len // LANES
    frame_len = framed.shape[1]
    width = 1024
    steps = bin_count // width

    def kernel(framed_ref, tmpl_ref, out_ref, taps_ref, shifted_ref):
        step = pl.program_id(0)

        @pl.when(step == 0)
        def _():
            row = lax.broadcasted_iota(jnp.int32, (LANES, LANES), 0)
            col = lax.broadcasted_iota(jnp.int32, (LANES, LANES), 1)
            flip = (row + col == LANES - 1).astype(jnp.bfloat16)
            for b in range(blocks):
                cut = slice(b * LANES, (b + 1) * LANES)
                real = jnp.dot(tmpl_ref[0, :, cut], flip, preferred_element_type=jnp.float32)
                imag = jnp.dot(tmpl_ref[1, :, cut], flip, preferred_element_type=jnp.float32)
                taps_ref[b, :tmpl_count, :LANES] = real.astype(jnp.bfloat16)
                taps_ref[b, :tmpl_count, LANES:] = (-imag).astype(jnp.bfloat16)
                taps_ref[b, tmpl_count:, :LANES] = imag.astype(jnp.bfloat16)
                taps_ref[b, tmpl_count:, LANES:] = real.astype(jnp.bfloat16)
            for part in range(2):
                spread = jnp.broadcast_to(framed_ref[part : part + 1, :], (8, frame_len))
                base = pltpu.roll(spread, 0, 1, stride=1, stride_axis=0)
                for g in range(LANES // 16):
                    lower = base if g == 0 else pltpu.roll(base, 16 * g, 1)
                    upper = pltpu.roll(base, 16 * g + 8, 1)
                    start = part * LANES + 16 * g
                    shifted_ref[start : start + 16, :] = jnp.concatenate(
                        [lower, upper], axis=0
                    ).astype(jnp.bfloat16)

        total = jnp.zeros((2 * tmpl_count, width), jnp.float32)
        for b in range(blocks):
            first = pl.multiple_of(step * width + (b + 1) * LANES, LANES)
            total = total + jnp.dot(
                taps_ref[b], shifted_ref[:, pl.ds(first, width)], preferred_element_type=jnp.float32
            )
        out_ref[0] = jnp.square(total[:tmpl_count]) + jnp.square(total[tmpl_count:])

    return pl.pallas_call(
        kernel,
        out_shape=jax.ShapeDtypeStruct((1, tmpl_count, bin_count), jnp.float32),
        grid=(steps,),
        in_specs=[
            pl.BlockSpec((2, frame_len), lambda i: (0, 0)),
            pl.BlockSpec(templates.shape, lambda i: (0, 0, 0)),
        ],
        out_specs=pl.BlockSpec((1, tmpl_count, width), lambda i: (0, 0, i)),
        scratch_shapes=[
            pltpu.VMEM((blocks, 2 * tmpl_count, 2 * LANES), jnp.bfloat16),
            pltpu.VMEM((2 * LANES, frame_len), jnp.bfloat16),
        ],
        compiler_params=pltpu.CompilerParams(vmem_limit_bytes=48 << 20),
    )(framed, templates)


def local(samples, clip_mask, delays, templates):
    return search(dedisperse(samples, clip_mask, delays), templates)


def search(whole, templates):
    row_count, inner_len = whole.shape
    total_len = row_count * inner_len
    bin_cols = SEARCH // row_count
    scale_bins = 1.0 / math.sqrt(total_len)
    outer_cos, outer_sin = phase_table(counting(row_count), counting(row_count), row_count)
    table_outer = jnp.concatenate([outer_cos, -outer_sin], axis=0)
    hold_cos, hold_sin = phase_table(counting(row_count), counting(inner_len), total_len)
    own_cols = bin_cols // lax.axis_size("band")
    folded = jnp.dot(table_outer, whole, precision=fine)
    fold_real = folded[:row_count]
    fold_imag = folded[row_count:]
    hold_real = fold_real * hold_cos + fold_imag * hold_sin
    hold_imag = fold_imag * hold_cos - fold_real * hold_sin
    half_taps = templates.shape[2] // 2
    side_cols = -(-half_taps // row_count)
    cols = lax.axis_index("band") * own_cols - side_cols + counting(own_cols + 2 * side_cols)
    last_cos, last_sin = phase_table(counting(inner_len), cols % inner_len, inner_len)
    inside = ((cols >= 0) & (cols < bin_cols)).astype(jnp.float32) * scale_bins
    last_cos = last_cos * inside
    last_sin = last_sin * inside
    table_last = jnp.concatenate(
        [
            jnp.concatenate([last_cos, -last_sin], axis=1),
            jnp.concatenate([last_sin, last_cos], axis=1),
        ],
        axis=0,
    )
    out = jnp.dot(jnp.concatenate([hold_real, hold_imag], axis=1), table_last, precision=fine)
    ordered = out.T.reshape(2, -1)
    local_bins = own_cols * row_count
    skip = side_cols * row_count - half_taps
    if skip:
        framed = ordered[:, skip - 1 : skip - 1 + local_bins + 2 * half_taps]
    else:
        framed = jnp.pad(ordered[:, :-1], ((0, 0), (1, 0)))
    return correlate(framed, templates, local_bins)


def solution(mesh):
    in_specs = (P(("beam", "band"), "tm"), P(("beam", "band"), "tm"), P(None, "band"), P())
    out_specs = P(("beam", "tm"), None, "band")
    return jax.shard_map(local, mesh=mesh, in_specs=in_specs, out_specs=out_specs, check_vma=False)
```

time: 52.6 us -> 62.3 us (1.18)
  Pallas kernels: 43.9 us -> 58.4 us
  local copies, waits for them, and re-layouts: 5.02 us -> 0.19 us
    pallas_call x2 -> x1, Pallas kernels: 35.5 us -> 49.7 us  [dedisperse(): pl.pallas_call(kernel, out_shape=jax.ShapeDtypeStruct((tm_count * rows, L...]
    unnamed x8 -> x2, local copies, waits for them, and re-layouts: 4.84 us -> 0.01 us
where the time goes in v1:
time: 62.3 us; the launch traced here: 61.9 us
  Pallas kernels  58.4 us (94%)
  other arithmetic  1.78 us (3%)
  matrix products  1.53 us (2%)
    pallas_call x1, Pallas kernels, dedisperse(): pl.pallas_call(kernel, out_shape=jax.ShapeDtypeStruct((tm_count * rows, L...  49.7 us
    pallas_call x1, Pallas kernels, correlate(): pl.pallas_call(kernel, out_shape=jax.ShapeDtypeStruct((1, tmpl_count, bin...  8.64 us
    dot_general x1, matrix products, search(): folded = jnp.dot(table_outer, whole, precision=fine)  1.32 us

profile of v1, /device:TPU:0, one launch (start us, length us, event | category | flops | bytes accessed | tf_op | source)
XLA Modules:
  0.0 61.9 jit_solution(3200472973308939399)
XLA Ops:
  0.0 0.0 copy-start
  0.0 0.2 fusion.36
  0.2 49.7 %shard_map.46 = f32[256,128]{1,0:T(8,128)} custom-call(s32[8,512]{1,0:T(8,128)} %lag_ref.1, s32[8,512]{1,0:T(8,128)} %lag_ref.1, bf16[512,4096]{1,0:T(8,128)(2,1)} %sample_ref.1, s32[32,512]{1,0:T(8,128)} %bitcast.4), custom_call_target="tpu_custom_call" | custom-call | tf_op jit(solution)/shard_map/pallas_call | solution.py:224
  49.9 1.0 %sine_negate_fusion = (f32[256,256]{1,0:T(8,128)S(1)}, f32[256,256]{1,0:T(8,128)S(1)}) fusion(), kind=kLoop, calls=%fused_computation.14 | loop fusion | flops 983040 | bytes 524288 | tf_op jit(solution)/shard_map/neg | solution.py:323
  51.0 1.3 %fusion = f32[512,128]{0,1:T(8,128)S(1)} fusion(f32[256,128]{1,0:T(8,128)} %shard_map.46, f32[256,256]{1,0:T(8,128)S(1)} %get-tuple-element.10, f32[256,256]{1,0:T(8,128)S(1)} %get-tuple-element.11), kind=kOutput, calls=%fused_computation | convolution fusion | flops 100794368 | bytes 917504 | tf_op jit(solution)/shard_map/dot_general | solution.py:326
  52.3 0.6 multiply_add_fusion
  52.9 0.2 fusion.7
  53.1 0.1 pad.4.framed_ref
  53.3 0.0 copy-done
  53.3 8.6 %shard_map.47 = f32[1,64,8192]{2,1,0:T(8,128)} custom-call(f32[2,9216]{1,0:T(2,128)S(1)} %pad.4.framed_ref, bf16[2,64,1024]{2,1,0:T(8,128)(2,1)S(1)} %copy-done), custom_call_target="tpu_custom_call" | custom-call | tf_op jit(solution)/shard_map/pallas_call | solution.py:296
  (3 shorter events, 0.1 us)
Async XLA Ops:
  0.0 53.3 %copy-start = (bf16[2,64,1024]{2,1,0:T(8,128)(2,1)S(1)}, bf16[2,64,1024]{2,1,0:T(8,128)(2,1)}, u32[]{:S(2)}) copy-start(bf16[2,64,1024]{2,1,0:T(8,128)(2,1)} %tmpl_ref.1) | copy-start | bytes 786436

commit v2 on v1

--- a/solution.py
+++ b/solution.py
@@ -40,7 +40,7 @@
     width = 2 * LANES
     chunks = slab_len // width
     group = width // rows
-    block = 64
+    held_back = min(8, chan_count // group - 1)
     spans = chan_count // LANES
     padded_rows = 2 * rows
 
@@ -122,8 +122,8 @@
         lax.fori_loop(0, chan_count // 8, pack, 0)
 
         lane = lax.broadcasted_iota(jnp.int32, (rows, LANES), 1)
-        lane_half = lane.astype(jnp.float32).astype(jnp.bfloat16)
-        row_lane = lax.broadcasted_iota(jnp.int32, (1, LANES), 1)
+        from_end = (LANES - 1 - lane).astype(jnp.float32).astype(jnp.bfloat16)
+        row_lane = lax.broadcasted_iota(jnp.int32, (1, LANES), 1).astype(jnp.float32)
         sign = (1 - 2 * (lax.broadcasted_iota(jnp.int32, (padded_rows, LANES), 1) % 2)).astype(jnp.float32)
         apart = (
             lax.broadcasted_iota(jnp.int32, (padded_rows, width), 0)
@@ -144,45 +144,40 @@
         def one_dm(k, _):
             dm = lax.rem(me + 1 + k, tm_count)
 
-            def one_block(n, total):
-                @pl.when((n == 1) & (k == 1))
-                def _():
-                    pl.semaphore_wait(barrier, peers)
-
-                @pl.when((n == 1) & (k > 0))
-                def _():
-                    for j in range(band_count):
-                        piece(k - 1, j).start()
-
-                for b in range(block // group):
-                    turned = []
-                    for i in range(group):
-                        chan = n * block + b * group + i
-                        low = delay_ref[dm, chan] & (LANES - 1)
-                        start = pl.multiple_of(chan * rows, rows)
-                        edge = jnp.full((rows, LANES), (LANES - low).astype(jnp.float32)).astype(jnp.bfloat16)
-                        merged = jnp.where(
-                            lane_half < edge,
-                            same_ref[pl.ds(start, rows), :],
-                            before_ref[pl.ds(start, rows), :],
-                        )
-                        rolled = pltpu.roll(merged, low, 1)
-                        top = rolled[:16].astype(jnp.float32)[:1]
-                        carry_ref[pl.ds(chan, 1), :] = jnp.where(row_lane < low, top, 0.0)
-                        turned.append(rolled)
-                    place_in = pl.multiple_of(
-                        lax.rem(n * block + b * group, LANES) * rows, width
+            total = jnp.zeros((padded_rows, LANES), jnp.float32)
+            for n in range(chan_count // group):
+                if n == held_back:
+
+                    @pl.when(k == 1)
+                    def _():
+                        pl.semaphore_wait(barrier, peers)
+
+                    @pl.when(k > 0)
+                    def _():
+                        for j in range(band_count):
+                            piece(k - 1, j).start()
+
+                turned = []
+                for chan in range(n * group, (n + 1) * group):
+                    low = delay_ref[dm, chan] & (LANES - 1)
+                    low_float = low.astype(jnp.float32)
+                    cut = slice(chan * rows, (chan + 1) * rows)
+                    merged = jnp.where(
+                        from_end >= jnp.full((rows, LANES), low_float).astype(jnp.bfloat16),
+                        same_ref[cut],
+                        before_ref[cut],
                     )
-                    lags = lag_rows[(n * block) // LANES, pl.ds(dm, 1), pl.ds(place_in, width)]
-                    chosen = (apart == lags).astype(jnp.float32).astype(jnp.bfloat16)
-                    total = total + jnp.dot(
-                        chosen, jnp.concatenate(turned, axis=0), preferred_element_type=jnp.float32
-                    )
-                return total
-
-            total = lax.fori_loop(
-                0, chan_count // block, one_block, jnp.zeros((padded_rows, LANES), jnp.float32)
-            )
+                    rolled = pltpu.roll(merged, low, 1)
+                    top = rolled[:16].astype(jnp.float32)[:1]
+                    carry_ref[chan : chan + 1, :] = jnp.where(row_lane < low_float, top, 0.0)
+                    turned.append(rolled)
+                first = n * group % LANES * rows
+                lags = lag_rows[n * group // LANES, pl.ds(dm, 1), first : first + width]
+                chosen = (apart == lags).astype(jnp.float32).astype(jnp.bfloat16)
+                total = total + jnp.dot(
+                    chosen, jnp.concatenate(turned, axis=0), preferred_element_type=jnp.float32
+                )
+
             row = lax.broadcasted_iota(jnp.int32, (padded_rows, chan_count), 0)
             lags = lag_ref[pl.ds(dm, 1), :] >> lane_bits
             fix = (row == lags + rows).astype(jnp.float32) - (row == lags).astype(jnp.float32)

time: 62.3 us -> 39 us (0.63)
  Pallas kernels: 58.4 us -> 35.3 us
    pallas_call x1, Pallas kernels: 49.7 us -> 26.6 us  [dedisperse(): pl.pallas_call(kernel, out_shape=jax.ShapeDtypeStruct((tm_count * rows, L...]
where the time goes in v2:
time: 39 us; the launch traced here: 38.8 us
  Pallas kernels  35.3 us (91%)
  other arithmetic  1.78 us (5%)
  matrix products  1.53 us (4%)
    pallas_call x1, Pallas kernels, dedisperse(): pl.pallas_call(kernel, out_shape=jax.ShapeDtypeStruct((tm_count * rows, L...  26.6 us
    pallas_call x1, Pallas kernels, correlate(): pl.pallas_call(kernel, out_shape=jax.ShapeDtypeStruct((1, tmpl_count, bin...  8.64 us
    dot_general x1, matrix products, search(): folded = jnp.dot(table_outer, whole, precision=fine)  1.32 us
    neg x1, other arithmetic, search(): table_outer = jnp.concatenate([outer_cos, -outer_sin], axis=0)  1.05 us

profile of v2, /device:TPU:0, one launch (start us, length us, event | category | flops | bytes accessed | tf_op | source)
XLA Modules:
  0.0 38.8 jit_solution(16090666985997458920)
XLA Ops:
  0.0 0.0 copy-start
  0.0 0.2 fusion.36
  0.2 26.6 %shard_map.46 = f32[256,128]{1,0:T(8,128)} custom-call(s32[8,512]{1,0:T(8,128)} %lag_ref.1, s32[8,512]{1,0:T(8,128)} %lag_ref.1, bf16[512,4096]{1,0:T(8,128)(2,1)} %sample_ref.1, s32[32,512]{1,0:T(8,128)} %bitcast.4), custom_call_target="tpu_custom_call" | custom-call | tf_op jit(solution)/shard_map/pallas_call | solution.py:219
  26.8 1.0 %sine_negate_fusion = (f32[256,256]{1,0:T(8,128)S(1)}, f32[256,256]{1,0:T(8,128)S(1)}) fusion(), kind=kLoop, calls=%fused_computation.14 | loop fusion | flops 983040 | bytes 524288 | tf_op jit(solution)/shard_map/neg | solution.py:318
  27.9 1.3 %fusion = f32[512,128]{0,1:T(8,128)S(1)} fusion(f32[256,128]{1,0:T(8,128)} %shard_map.46, f32[256,256]{1,0:T(8,128)S(1)} %get-tuple-element.10, f32[256,256]{1,0:T(8,128)S(1)} %get-tuple-element.11), kind=kOutput, calls=%fused_computation | convolution fusion | flops 100794368 | bytes 917504 | tf_op jit(solution)/shard_map/dot_general | solution.py:321
  29.2 0.6 %multiply_add_fusion = (f32[256,128]{0,1:T(8,128)S(1)}, f32[256,128]{0,1:T(8,128)S(1)}) fusion(f32[512,128]{0,1:T(8,128)S(1)} %fusion), kind=kLoop, calls=%fused_computation.25 | loop fusion | flops 655360 | bytes 524288 | tf_op jit(solution)/shard_map/add | solution.py:324
  29.8 0.2 fusion.7
  30.0 0.1 pad.4.framed_ref
  30.2 0.0 copy-done
  30.2 8.6 %shard_map.47 = f32[1,64,8192]{2,1,0:T(8,128)} custom-call(f32[2,9216]{1,0:T(2,128)S(1)} %pad.4.framed_ref, bf16[2,64,1024]{2,1,0:T(8,128)(2,1)S(1)} %copy-done), custom_call_target="tpu_custom_call" | custom-call | tf_op jit(solution)/shard_map/pallas_call | solution.py:291
  (3 shorter events, 0.1 us)
Async XLA Ops:
  0.0 30.2 %copy-start = (bf16[2,64,1024]{2,1,0:T(8,128)(2,1)S(1)}, bf16[2,64,1024]{2,1,0:T(8,128)(2,1)}, u32[]{:S(2)}) copy-start(bf16[2,64,1024]{2,1,0:T(8,128)(2,1)} %tmpl_ref.1) | copy-start | bytes 786436

commit v3 on v2

--- a/solution.py
+++ b/solution.py
@@ -2,6 +2,7 @@
 
 import jax
 import jax.numpy as jnp
+import numpy as np
 from jax import lax
 from jax.experimental import pallas as pl
 from jax.experimental.pallas import tpu as pltpu
@@ -12,17 +13,6 @@
 LANES = 128
 
 clip_level = 2.5
-fine = lax.Precision.HIGH
-
-
-def counting(length):
-    return jnp.arange(length, dtype=jnp.int32)
-
-
-def phase_table(first_index, second_index, period):
-    turn_count = first_index[:, None] * second_index[None, :] % period
-    angles = turn_count.astype(jnp.float32) * (2.0 * math.pi / period)
-    return (jnp.cos(angles), jnp.sin(angles))
 
 
 def dedisperse(samples, clip_mask, delays):
@@ -241,19 +231,77 @@
             pltpu.SemaphoreType.DMA((dm_count, band_count)),
         ],
         compiler_params=pltpu.CompilerParams(
-            collective_id=0, has_side_effects=True, vmem_limit_bytes=56 << 20
+            collective_id=0, has_side_effects=True, vmem_limit_bytes=54 << 20
         ),
     )(delays, delays, samples, clip_mask.T)
 
 
-def correlate(framed, templates, bin_count):
+def halves(table):
+    high = table.astype(jnp.bfloat16)
+    low = (table - high.astype(np.float64)).astype(jnp.bfloat16)
+    return np.stack([high, low])
+
+
+def split(values):
+    high = values.astype(jnp.bfloat16)
+    return high, (values - high.astype(jnp.float32)).astype(jnp.bfloat16)
+
+
+def three_pass(left, right, dims):
+    def product(x, y):
+        return lax.dot_general(x, y, (dims, ((), ())), preferred_element_type=jnp.float32)
+
+    return product(left[0], right[1]) + product(left[1], right[0]) + product(left[0], right[0])
+
+
+def turn(first_index, second_index, period):
+    return (first_index[:, None] * second_index[None, :] % period) * (2.0 * math.pi / period)
+
+
+def search(whole, templates):
+    row_count, inner_len = whole.shape
+    total_len = row_count * inner_len
+    bin_cols = SEARCH // row_count
+    band_count = lax.axis_size("band")
+    own_cols = bin_cols // band_count
     tmpl_count, tap_len = templates.shape[1:]
+    half_taps = tap_len // 2
+    side_cols = -(-half_taps // row_count)
+    col_count = own_cols + 2 * side_cols
+    skip = side_cols * row_count - half_taps
+    bin_count = own_cols * row_count
+    frame_len = bin_count + tap_len
     blocks = tap_len // LANES
-    frame_len = framed.shape[1]
     width = 1024
     steps = bin_count // width
-
-    def kernel(framed_ref, tmpl_ref, out_ref, taps_ref, shifted_ref):
+    assert skip % LANES == 0
+
+    counts = np.arange(row_count)
+    inner = np.arange(inner_len)
+    outer = turn(counts, counts, row_count)
+    outer_table = halves(np.concatenate([np.cos(outer), -np.sin(outer)], axis=0))
+    hold = turn(counts, inner, total_len)
+    hold_table = np.stack([np.cos(hold), np.sin(hold)]).astype(np.float32)
+    last_tables = []
+    for b in range(band_count):
+        cols = b * own_cols - side_cols + np.arange(col_count)
+        angles = turn(cols % inner_len, inner, inner_len)
+        kept = ((cols >= 0) & (cols < bin_cols))[:, None] / math.sqrt(total_len)
+        cosine, sine = np.cos(angles) * kept, np.sin(angles) * kept
+        last_tables.append(
+            halves(
+                np.concatenate(
+                    [
+                        np.concatenate([cosine, sine], axis=1),
+                        np.concatenate([-sine, cosine], axis=1),
+                    ],
+                    axis=0,
+                )
+            )
+        )
+    last_table = np.stack(last_tables)
+
+    def kernel(whole_ref, outer_ref, hold_ref, last_ref, tmpl_ref, out_ref, framed_ref, taps_ref, shifted_ref):
         step = pl.program_id(0)
 
         @pl.when(step == 0)
@@ -269,9 +317,25 @@
                 taps_ref[b, :tmpl_count, LANES:] = (-imag).astype(jnp.bfloat16)
                 taps_ref[b, tmpl_count:, :LANES] = imag.astype(jnp.bfloat16)
                 taps_ref[b, tmpl_count:, LANES:] = real.astype(jnp.bfloat16)
+            folded = three_pass((outer_ref[0], outer_ref[1]), split(whole_ref[...]), ((1,), (0,)))
+            fold_real, fold_imag = folded[:row_count], folded[row_count:]
+            hold_cos, hold_sin = hold_ref[0], hold_ref[1]
+            held = jnp.concatenate(
+                [fold_real * hold_cos + fold_imag * hold_sin, fold_imag * hold_cos - fold_real * hold_sin],
+                axis=1,
+            )
+            band = lax.axis_index("band")
+            bins = three_pass((last_ref[band, 0], last_ref[band, 1]), split(held), ((1,), (1,)))
             for part in range(2):
-                spread = jnp.broadcast_to(framed_ref[part : part + 1, :], (8, frame_len))
-                base = pltpu.roll(spread, 0, 1, stride=1, stride_axis=0)
+                for i in range(col_count):
+                    framed_ref[part : part + 1, i * row_count : (i + 1) * row_count] = bins[
+                        part * col_count + i : part * col_count + i + 1
+                    ]
+            for part in range(2):
+                spread = jnp.broadcast_to(
+                    framed_ref[part : part + 1, skip : skip + frame_len], (8, frame_len)
+                )
+                base = pltpu.roll(spread, 1, 1, stride=1, stride_axis=0)
                 for g in range(LANES // 16):
                     lower = base if g == 0 else pltpu.roll(base, 16 * g, 1)
                     upper = pltpu.roll(base, 16 * g + 8, 1)
@@ -288,64 +352,28 @@
             )
         out_ref[0] = jnp.square(total[:tmpl_count]) + jnp.square(total[tmpl_count:])
 
+    def resident(array):
+        zeros = (0,) * array.ndim
+        return pl.BlockSpec(array.shape, lambda i: zeros)
+
+    operands = (whole, outer_table, hold_table, last_table, templates)
     return pl.pallas_call(
         kernel,
         out_shape=jax.ShapeDtypeStruct((1, tmpl_count, bin_count), jnp.float32),
         grid=(steps,),
-        in_specs=[
-            pl.BlockSpec((2, frame_len), lambda i: (0, 0)),
-            pl.BlockSpec(templates.shape, lambda i: (0, 0, 0)),
-        ],
+        in_specs=[resident(x) for x in operands],
         out_specs=pl.BlockSpec((1, tmpl_count, width), lambda i: (0, 0, i)),
         scratch_shapes=[
+            pltpu.VMEM((2, col_count * row_count), jnp.float32),
             pltpu.VMEM((blocks, 2 * tmpl_count, 2 * LANES), jnp.bfloat16),
             pltpu.VMEM((2 * LANES, frame_len), jnp.bfloat16),
         ],
         compiler_params=pltpu.CompilerParams(vmem_limit_bytes=48 << 20),
-    )(framed, templates)
+    )(*operands)
 
 
 def local(samples, clip_mask, delays, templates):
     return search(dedisperse(samples, clip_mask, delays), templates)
-
-
-def search(whole, templates):
-    row_count, inner_len = whole.shape
-    total_len = row_count * inner_len
-    bin_cols = SEARCH // row_count
-    scale_bins = 1.0 / math.sqrt(total_len)
-    outer_cos, outer_sin = phase_table(counting(row_count), counting(row_count), row_count)
-    table_outer = jnp.concatenate([outer_cos, -outer_sin], axis=0)
-    hold_cos, hold_sin = phase_table(counting(row_count), counting(inner_len), total_len)
-    own_cols = bin_cols // lax.axis_size("band")
-    folded = jnp.dot(table_outer, whole, precision=fine)
-    fold_real = folded[:row_count]
-    fold_imag = folded[row_count:]
-    hold_real = fold_real * hold_cos + fold_imag * hold_sin
-    hold_imag = fold_imag * hold_cos - fold_real * hold_sin
-    half_taps = templates.shape[2] // 2
-    side_cols = -(-half_taps // row_count)
-    cols = lax.axis_index("band") * own_cols - side_cols + counting(own_cols + 2 * side_cols)
-    last_cos, last_sin = phase_table(counting(inner_len), cols % inner_len, inner_len)
-    inside = ((cols >= 0) & (cols < bin_cols)).astype(jnp.float32) * scale_bins
-    last_cos = last_cos * inside
-    last_sin = last_sin * inside
-    table_last = jnp.concatenate(
-        [
-            jnp.concatenate([last_cos, -last_sin], axis=1),
-            jnp.concatenate([last_sin, last_cos], axis=1),
-        ],
-        axis=0,
-    )
-    out = jnp.dot(jnp.concatenate([hold_real, hold_imag], axis=1), table_last, precision=fine)
-    ordered = out.T.reshape(2, -1)
-    local_bins = own_cols * row_count
-    skip = side_cols * row_count - half_taps
-    if skip:
-        framed = ordered[:, skip - 1 : skip - 1 + local_bins + 2 * half_taps]
-    else:
-        framed = jnp.pad(ordered[:, :-1], ((0, 0), (1, 0)))
-    return correlate(framed, templates, local_bins)
 
 
 def solution(mesh):

time: 39 us -> 37 us (0.949)
  other arithmetic: 1.78 us -> 0 us
  matrix products: 1.53 us -> 0 us
  local copies, waits for them, and re-layouts: 0.19 us -> 0.91 us
  Pallas kernels: 35.3 us -> 35.9 us
    dot_general x2 -> x0, matrix products: 1.53 us -> none  [the longest x1 1.32 us: search(): folded = jnp.dot(table_outer, whole, precision=fine)]
    neg x2 -> x0, other arithmetic: 1.21 us -> none  [the longest x1 1.05 us: search(): table_outer = jnp.concatenate([outer_cos, -outer_sin], axis=0)]
    unnamed x2 -> x10, local copies, waits for them, and re-layouts: 0.01 us -> 0.91 us
    add x1 -> x0, other arithmetic: 0.56 us -> none  [search(): hold_real = fold_real * hold_cos + fold_imag * hold_sin]
    pallas_call x1, Pallas kernels: 8.64 us -> 9.08 us  [search(): pl.pallas_call(kernel, out_shape=jax.ShapeDtypeStruct((1, tmpl_count, bin...]
where the time goes in v3:
time: 37 us; the launch traced here: 36.8 us
  Pallas kernels  35.9 us (97%)
  local copies, waits for them, and re-layouts  0.91 us (2%)
    pallas_call x1, Pallas kernels, dedisperse(): pl.pallas_call(kernel, out_shape=jax.ShapeDtypeStruct((tm_count * rows, L...  26.8 us
    pallas_call x1, Pallas kernels, search(): pl.pallas_call(kernel, out_shape=jax.ShapeDtypeStruct((1, tmpl_count, bin...  9.08 us
    unnamed x10, local copies, waits for them, and re-layouts  0.91 us

profile of v3, /device:TPU:0, one launch (start us, length us, event | category | flops | bytes accessed | tf_op | source)
XLA Modules:
  0.0 36.8 jit_solution(15330224563525638462)
XLA Ops:
  0.0 0.0 copy-start.4
  0.0 0.0 copy-start.3
  0.0 0.0 copy-start
  0.0 0.0 copy-start.2
  0.0 26.8 %shard_map.73.whole_ref = f32[256,128]{1,0:T(8,128)} custom-call(s32[8,512]{1,0:T(8,128)} %lag_ref.1, s32[8,512]{1,0:T(8,128)} %lag_ref.1, bf16[512,4096]{1,0:T(8,128)(2,1)} %sample_ref.1, s32[32,512]{1,0:T(8,128)} %bitcast.1), custom_call_target="tpu_custom_call" | custom-call | tf_op jit(solution)/shard_map/pallas_call | solution.py:209
  26.8 0.0 copy-done.4
  26.8 0.0 copy-done.3
  26.8 0.0 copy-done
  26.8 0.0 copy-done.2
  26.8 0.0 copy-start.1
  26.8 0.9 %copy-done.1 = f32[256,128]{1,0:T(8,128)S(1)} copy-done((f32[256,128]{1,0:T(8,128)S(1)}, f32[256,128]{1,0:T(8,128)}, u32[]{:S(2)}) %copy-start.1) | copy-done | bytes 131096
  27.7 9.1 %shard_map.74 = f32[1,64,8192]{2,1,0:T(8,128)} custom-call(f32[256,128]{1,0:T(8,128)S(1)} %copy-done.1, bf16[2,512,256]{2,1,0:T(8,128)(2,1)S(1)} %copy-done, f32[2,256,128]{2,1,0:T(8,128)S(1)} %copy-done.3, bf16[2,2,72,256]{3,2,1,0:T(8,128)(2,1)S(1)} %copy-done.4, bf16[2,64,1024]{2,1,0:T(8,128)(2,1)S(1)} %copy-done.2), custom_call_target="tpu_custom_call" | custom-call | tf_op jit(solution)/shard_map/pallas_call | solution.py:360
Async XLA Ops:
  0.0 26.8 %copy-start.4 = (bf16[2,2,72,256]{3,2,1,0:T(8,128)(2,1)S(1)}, bf16[2,2,72,256]{3,2,1,0:T(8,128)(2,1)}, u32[]{:S(2)}) copy-start(bf16[2,2,72,256]{3,2,1,0:T(8,128)(2,1)} %constant.8.clone.last_ref) | copy-start | bytes 442372
  0.0 26.8 %copy-start.3 = (f32[2,256,128]{2,1,0:T(8,128)S(1)}, f32[2,256,128]{2,1,0:T(8,128)}, u32[]{:S(2)}) copy-start(f32[2,256,128]{2,1,0:T(8,128)} %constant.7.clone.hold_ref) | copy-start | bytes 786436
  0.0 26.8 %copy-start = (bf16[2,512,256]{2,1,0:T(8,128)(2,1)S(1)}, bf16[2,512,256]{2,1,0:T(8,128)(2,1)}, u32[]{:S(2)}) copy-start(bf16[2,512,256]{2,1,0:T(8,128)(2,1)} %constant.6.clone.outer_ref) | copy-start | bytes 1572868
  0.0 26.8 %copy-start.2 = (bf16[2,64,1024]{2,1,0:T(8,128)(2,1)S(1)}, bf16[2,64,1024]{2,1,0:T(8,128)(2,1)}, u32[]{:S(2)}) copy-start(bf16[2,64,1024]{2,1,0:T(8,128)(2,1)} %tmpl_ref.1) | copy-start | bytes 786436
  26.8 0.9 %copy-start.1 = (f32[256,128]{1,0:T(8,128)S(1)}, f32[256,128]{1,0:T(8,128)}, u32[]{:S(2)}) copy-start(f32[256,128]{1,0:T(8,128)} %shard_map.73.whole_ref) | copy-start | bytes 393220
